TPU v7x, 32 devices: a whole 2x2x4 slice. The times are simulated.
32 devices in a mesh: row: 4 (over y, x), col: 8 (over z, core).
Axes of the slice: x: 2, y: 2, z: 4, core: 2. Of those that a mesh axis runs over, the one named last changes fastest.
Arguments:
- velocities: bfloat16 [1024, 30720], P(None, 'row'), may hold values from -60 to 60, as said below
- modes_panel: bfloat16 [30720, 4096], P('row', 'col'), may hold values from -1 to 1
- atom_slot: int32 [10240], P('row'), may hold values from 0 to 2559, as said below
- lag_offsets: int32 [8], replicated, may hold values from 0 to 256, as said below
Outputs:
- correlations: float32 [8, 4096, 4096], P(None, 'row', 'col')
Inputs may be any that keep to these rules, and one draw needn't show every extreme that they name: `velocities`: every snapshot row has its own scale. Within each aligned block of 2560 atoms, atom_slot is a permutation of 0 to 2559. `lag_offsets`: one of the lags equals 256.
All inputs are finite; a program needn't handle non-finite values.
Results may differ from a plain program's by a relative error of at most 0.0041.
Values may be sent and summed in bfloat16 or wider, within the bound.
No kernel may reach another device: no remote copies, remote signals or barrier semaphores. Data moves between devices by JAX's collectives and lax.ppermute only.
A program may use at most 128 MiB of HBM per device.

v0:
```python
import jax
import jax.numpy as jnp
from jax import lax
from jax.sharding import PartitionSpec as P

M = 4096
LAGS = 8
MAXLAG = 256
epsilon = 1e-06


def from_root(block, axis, owner):
    block = jnp.where(lax.axis_index(axis) == owner, block, jnp.zeros_like(block))
    return lax.psum(block, axis)


def reorder(modes_panel, atom_slot):
    per_atom = modes_panel.reshape(atom_slot.shape[0], 3, modes_panel.shape[1])
    return jnp.take(per_atom, atom_slot, axis=0).reshape(modes_panel.shape)


def correlate(row_modes, column_modes, lag_offsets):
    snapshots = column_modes.shape[0]
    padded = jnp.concatenate(
        [column_modes, jnp.zeros((MAXLAG, column_modes.shape[1]), jnp.bfloat16)], axis=0
    )
    results = []
    for number in range(LAGS):
        offset = lag_offsets[number]
        shifted = lax.dynamic_slice_in_dim(padded, offset, snapshots, 0)
        product = lax.dot_general(
            row_modes, shifted, (((0,), (0,)), ((), ())), preferred_element_type=jnp.float32
        )
        results.append(product * lax.rsqrt((snapshots - offset).astype(jnp.float32)))
    return jnp.stack(results)


def local(velocities, modes_panel, atom_slot, lag_offsets):
    panel = reorder(modes_panel, atom_slot)
    row_count = lax.axis_size("row")
    col_count = lax.axis_size("col")
    partial_terms = jnp.dot(velocities, panel, preferred_element_type=jnp.float32)
    projected = lax.psum(partial_terms, "row")
    energy = lax.psum(jnp.sum(projected * projected, axis=1), "col")
    column_modes = (projected * lax.rsqrt(energy / M + epsilon)[:, None]).astype(jnp.bfloat16)
    owners = col_count // row_count
    pieces = [
        from_root(column_modes, "col", lax.axis_index("row") * owners + owner)
        for owner in range(owners)
    ]
    row_modes = jnp.concatenate(pieces, axis=1)
    return correlate(row_modes, column_modes, lag_offsets)


def solution(mesh):
    return jax.shard_map(
        local,
        mesh=mesh,
        in_specs=(P(None, "row"), P("row", "col"), P("row"), P()),
        out_specs=P(None, "row", "col"),
        check_vma=False,
    )
```

profile of v0, /device:TPU:0, one launch (start us, length us, event | category | flops | bytes accessed | tf_op | source)
XLA Modules:
  0.0 267.6 jit_solution(14538257471376262001)
XLA Ops:
  6.5 0.7 compare_select_fusion
  7.2 0.7 compare_and_fusion
  8.0 20.7 %reshape.12 = bf16[2560,3,512]{2,1,0:T(4,128)(2,1)} reshape(bf16[7680,512]{1,0:T(8,128)(2,1)} %param.5) | data formatting | bytes 15728640 | tf_op jit(solution)/shard_map/reshape | solution.py:18
  28.7 17.1 %gather_fusion = bf16[2560,3,512]{2,1,0:T(4,128)(2,1)} fusion(bf16[2560,3,512]{2,1,0:T(4,128)(2,1)} %reshape.12, s32[3072]{0:T(1024)S(1)} %pad_clamp_fusion), kind=kCustom, calls=%fused_computation | custom fusion | bytes 15738880 | tf_op jit(solution)/shard_map/jit(_take)/gather | solution.py:19
  45.9 20.0 %gather.7 = bf16[7680,512]{1,0:T(8,128)(2,1)} reshape(bf16[2560,3,512]{2,1,0:T(4,128)(2,1)} %gather_fusion) | data formatting | bytes 15728640 | tf_op jit(solution)/shard_map/jit(_take)/gather | solution.py:19
  65.9 1.3 broadcast_in_dim.18
  67.2 1.1 broadcast_in_dim.19
  68.3 16.5 %fusion.4 = f32[1024,512]{0,1:T(8,128)} fusion(bf16[1024,7680]{1,0:T(8,128)(2,1)} %param.4, bf16[7680,512]{1,0:T(8,128)(2,1)} %gather.7, pred[7680]{0:T(1024)(128)(4,1)S(1)} %broadcast_in_dim.19), kind=kOutput, calls=%fused_computation.15 | convolution fusion | flops 8056995840 | bytes 25697792 | tf_op jit(solution)/shard_map/dot_general | solution.py:42
  84.9 72.3 %all-reduce.5.cloned.1.call-done = f32[1024,512]{0,1:T(8,128)} async-done(((f32[1024,512]{0,1:T(8,128)}), f32[1024,512]{0,1:T(8,128)}) %all-reduce.5.cloned.1.call-update) | async-done | bytes 2097168 | tf_op jit(solution)/shard_map/psum | solution.py:43
  157.2 1.9 multiply_reduce_fusion
  159.1 16.4 %psum.29 = f32[1024]{0:T(1024)S(1)} all-reduce(f32[1024]{0:T(1024)S(1)} %multiply_reduce_fusion), channel_id=1, replica_groups=mesh['row'=4,'col'=8] {'col'}, use_global_device_ids=true, to_apply=%region_2.3 | all-reduce | flops 1024 | bytes 8192 | tf_op jit(solution)/shard_map/psum | solution.py:44
  175.5 1.4 broadcast_select_fusion
  176.9 1.1 broadcast_select_fusion.1
  198.4 42.2 %all-reduce.7.cloned.1.call-done = (bf16[1024,512]{0,1:T(8,128)(2,1)}, bf16[1024,512]{0,1:T(8,128)(2,1)}) async-done(((bf16[1024,512]{0,1:T(8,128)(2,1)}, bf16[1024,512]{0,1:T(8,128)(2,1)}), (bf16[1024,512]{0,1:T(8,128)(2,1)}, bf16[1024,512]{0,1:T(8,128)(2,1)})) %all-reduce.7.cloned.1.call-update) | async-done | bytes 2097168 | tf_op jit(solution)/shard_map/psum | solution.py:14
  240.6 1.4 constant_dynamic-update-slice_fusion.1
  242.2 1.4 bitcast_dynamic-update-slice_fusion.7
  243.6 1.4 bitcast_dynamic-update-slice_fusion.6
  245.0 1.4 bitcast_dynamic-update-slice_fusion.5
  246.4 1.4 bitcast_dynamic-update-slice_fusion.4
  247.8 1.4 bitcast_dynamic-update-slice_fusion.3
  249.1 1.4 bitcast_dynamic-update-slice_fusion.2
  250.5 1.4 bitcast_dynamic-update-slice_fusion.1
  251.9 6.2 %copy-done.3 = f32[8,1024,512]{2,1,0:T(8,128)} copy-done((f32[8,1024,512]{2,1,0:T(8,128)}, f32[8,1024,512]{2,1,0:T(8,128)S(1)}, u32[]{:S(2)}) %copy-start.3) | copy-done | bytes 16777240
  258.1 2.7 %bitcast_dynamic-update-slice_fusion = f32[8,1024,512]{2,1,0:T(8,128)} fusion(f32[8,1024,512]{2,1,0:T(8,128)} %copy-done.3, bf16[1024,1024]{0,1:T(8,128)(2,1)S(1)} %constant_dynamic-update-slice_fusion, s32[]{:T(128)S(6)} %select_n.61, bf16[1024,512]{0,1:T(8,128)(2,1)S(1)} %get-tuple-element.8, f32[]{:T(128)S(6)} %rsqrt.35), kind=kOutput, calls=%fused_computation.5 | convolution fusion | flops 1074266112 | bytes 5242888 | tf_op jit(solution)/shard_map/dot_general | solution.py:31
  (15 shorter events, 1.0 us)
Async XLA Ops:
  6.5 150.7 %all-reduce.5.cloned.1.call-start = ((), (), s32[]{:S(2)}) async-start(), calls=%async_computation | async-start | bytes 4194304 | tf_op jit(solution)/shard_map/psum | solution.py:43
  84.9 155.8 %all-reduce.7.cloned.1.call-start = ((), (), s32[]{:S(2)}) async-start(), calls=%async_computation.1 | async-start | bytes 4194304 | tf_op jit(solution)/shard_map/psum | solution.py:14
  157.2 18.3 %copy-start = (f32[1024,512]{0,1:T(8,128)S(1)}, f32[1024,512]{0,1:T(8,128)}, u32[]{:S(2)}) copy-start(f32[1024,512]{0,1:T(8,128)} %all-reduce.5.cloned.1.call-done) | copy-start | bytes 6291460
  176.9 1.1 copy-start.2
  240.6 1.5 copy-start.1
  251.9 6.2 %copy-start.3 = (f32[8,1024,512]{2,1,0:T(8,128)}, f32[8,1024,512]{2,1,0:T(8,128)S(1)}, u32[]{:S(2)}) copy-start(f32[8,1024,512]{2,1,0:T(8,128)S(1)} %bitcast_dynamic-update-slice_fusion.1) | copy-start | bytes 50331652
Sparse Core Ops, SparseCore 0:
  85.0 72.1 all-reduce.4
  178.1 62.4 all-reduce.6
where the time goes:
time: 269 us; the launch traced here: 268 us
  waiting for transfers between devices  115 us (43%)
  local copies, waits for them, and re-layouts  68.8 us (26%)
  between operations  33.2 us (12%)
  matrix products  28.9 us (11%)
  blocking collectives  16.4 us (6%)
  other arithmetic  5.85 us (2%)
    psum x1, waiting for transfers between devices, local(): projected = lax.psum(partial_terms, 'row')  72.3 us
    psum x1, waiting for transfers between devices, from_root(): return lax.psum(block, axis)  42.2 us
    gather x2, local copies, waits for them, and re-layouts, reorder(): return jnp.take(per_atom, atom_slot, axis=0).reshape(modes_panel.shape)  37.2 us
    reshape x1, local copies, waits for them, and re-layouts, reorder(): per_atom = modes_panel.reshape(atom_slot.shape[0], 3, modes_panel.shape[1])  20.7 us
    dot_general x1, matrix products, local(): jnp.dot(velocities, panel, preferred_element_type=jnp.float32)  16.5 us
    psum x1, blocking collectives, local(): energy = lax.psum(jnp.sum(projected * projected, axis=1), 'col')  16.4 us
    dot_general x8, matrix products, correlate(): lax.dot_general(row_modes, shifted, (((0,), (0,)), ((), ())), preferred_e...  12.3 us
    unnamed x9, local copies, waits for them, and re-layouts  7.7 us
  transfers between devices with their start and end apart: 2, of which 2 were waited for; matrix products, arithmetic and copies ran while one was open for 0% of the time, Pallas kernels for 0%

commit v1 on v0

--- a/solution.py
+++ b/solution.py
@@ -40,7 +40,7 @@
     row_count = lax.axis_size("row")
     col_count = lax.axis_size("col")
     partial_terms = jnp.dot(velocities, panel, preferred_element_type=jnp.float32)
-    projected = lax.psum(partial_terms, "row")
+    projected = jnp.sum(lax.all_gather(partial_terms, "row"), axis=0)
     energy = lax.psum(jnp.sum(projected * projected, axis=1), "col")
     column_modes = (projected * lax.rsqrt(energy / M + epsilon)[:, None]).astype(jnp.bfloat16)
     owners = col_count // row_count

time: 269 us -> 305 us (1.13)
  waiting for transfers between devices: 115 us -> 132 us
  local copies, waits for them, and re-layouts: 68.8 us -> 79.6 us
  other arithmetic: 5.85 us -> 12.6 us
    all_gather x0 -> x1, waiting for transfers between devices: none -> 90.1 us  [local(): projected = jnp.sum(lax.all_gather(partial_terms, 'row'), axis=0)]
    psum x1 -> x0, waiting for transfers between devices: 72.3 us -> none  [local(): projected = lax.psum(partial_terms, 'row')]
    all_gather x0 -> x1, local copies, waits for them, and re-layouts: none -> 10.8 us  [local(): projected = jnp.sum(lax.all_gather(partial_terms, 'row'), axis=0)]
    reduce_sum x0 -> x1, other arithmetic: none -> 8.49 us  [local(): projected = jnp.sum(lax.all_gather(partial_terms, 'row'), axis=0)]
    unnamed x9 -> x7, local copies, waits for them, and re-layouts: 7.7 us -> 7.7 us
where the time goes in v1:
time: 305 us; the launch traced here: 303 us
  waiting for transfers between devices  132 us (43%)
  local copies, waits for them, and re-layouts  79.6 us (26%)
  between operations  33.5 us (11%)
  matrix products  28.9 us (9%)
  blocking collectives  16.4 us (5%)
  other arithmetic  12.6 us (4%)
    all_gather x1, waiting for transfers between devices, local(): projected = jnp.sum(lax.all_gather(partial_terms, 'row'), axis=0)  90.1 us
    psum x1, waiting for transfers between devices, from_root(): return lax.psum(block, axis)  42 us
    gather x2, local copies, waits for them, and re-layouts, reorder(): return jnp.take(per_atom, atom_slot, axis=0).reshape(modes_panel.shape)  37.2 us
    reshape x1, local copies, waits for them, and re-layouts, reorder(): per_atom = modes_panel.reshape(atom_slot.shape[0], 3, modes_panel.shape[1])  20.7 us
    dot_general x1, matrix products, local(): jnp.dot(velocities, panel, preferred_element_type=jnp.float32)  16.6 us
    psum x1, blocking collectives, local(): energy = lax.psum(jnp.sum(projected * projected, axis=1), 'col')  16.4 us
    dot_general x8, matrix products, correlate(): lax.dot_general(row_modes, shifted, (((0,), (0,)), ((), ())), preferred_e...  12.3 us
    all_gather x1, local copies, waits for them, and re-layouts, local(): projected = jnp.sum(lax.all_gather(partial_terms, 'row'), axis=0)  10.8 us
  transfers between devices with their start and end apart: 2, of which 2 were waited for; matrix products, arithmetic and copies ran while one was open for 0% of the time, Pallas kernels for 0%

profile of v1, /device:TPU:0, one launch (start us, length us, event | category | flops | bytes accessed | tf_op | source)
XLA Modules:
  0.0 303.4 jit_solution(16072786743712452493)
XLA Ops:
  7.2 0.7 compare_and_fusion
  8.0 20.7 %reshape.12 = bf16[2560,3,512]{2,1,0:T(4,128)(2,1)} reshape(bf16[7680,512]{1,0:T(8,128)(2,1)} %param.5) | data formatting | bytes 15728640 | tf_op jit(solution)/shard_map/reshape | solution.py:18
  28.7 17.2 %gather_fusion = bf16[2560,3,512]{2,1,0:T(4,128)(2,1)} fusion(bf16[2560,3,512]{2,1,0:T(4,128)(2,1)} %reshape.12, s32[3072]{0:T(1024)S(1)} %pad_clamp_fusion), kind=kCustom, calls=%fused_computation | custom fusion | bytes 15738880 | tf_op jit(solution)/shard_map/jit(_take)/gather | solution.py:19
  45.9 20.0 %gather.7 = bf16[7680,512]{1,0:T(8,128)(2,1)} reshape(bf16[2560,3,512]{2,1,0:T(4,128)(2,1)} %gather_fusion) | data formatting | bytes 15728640 | tf_op jit(solution)/shard_map/jit(_take)/gather | solution.py:19
  65.9 1.3 broadcast_in_dim.18
  67.2 1.1 broadcast_in_dim.19
  68.3 16.6 %fusion.4 = f32[1024,512]{0,1:T(8,128)} fusion(bf16[1024,7680]{1,0:T(8,128)(2,1)} %param.4, bf16[7680,512]{1,0:T(8,128)(2,1)} %gather.7, pred[7680]{0:T(1024)(128)(4,1)S(1)} %broadcast_in_dim.19), kind=kOutput, calls=%fused_computation.15 | convolution fusion | flops 8056995840 | bytes 25697792 | tf_op jit(solution)/shard_map/dot_general | solution.py:42
  85.2 90.1 %all-gather.3.cloned.1.call-done = f32[4096,512]{0,1:T(8,128)} async-done(((f32[1024,512]{0,1:T(8,128)}), f32[4096,512]{0,1:T(8,128)}) %all-gather.3.cloned.1.call-update) | async-done | bytes 8388624 | tf_op jit(solution)/shard_map/all_gather | solution.py:43
  175.3 10.8 %reshape.21 = f32[4,1024,512]{1,0,2:T(4,128)} reshape(f32[4096,512]{0,1:T(8,128)} %all-gather.3.cloned.1.call-done) | data formatting | bytes 16777216 | tf_op jit(solution)/shard_map/all_gather | solution.py:43
  186.1 8.5 %reduce_sum.18 = f32[1024,512]{0,1:T(8,128)S(1)} reduce(f32[4,1024,512]{1,0,2:T(4,128)} %reshape.21, f32[]{:T(128)} %constant.12.clone.1), dimensions={0}, to_apply=%region_0.1 | reduce | flops 1572864 | bytes 10485764 | tf_op jit(solution)/shard_map/reduce_sum | solution.py:43
  194.8 16.4 %psum.21 = f32[1024]{0:T(1024)S(1)} all-reduce(f32[1024]{0:T(1024)S(1)} %multiply_reduce_fusion), channel_id=1, replica_groups=mesh['row'=4,'col'=8] {'col'}, use_global_device_ids=true, to_apply=%region_2.3 | all-reduce | flops 1024 | bytes 8192 | tf_op jit(solution)/shard_map/psum | solution.py:44
  211.2 1.4 broadcast_select_fusion
  212.6 1.1 broadcast_select_fusion.1
  234.4 42.0 %all-reduce.4.cloned.1.call-done = (bf16[1024,512]{0,1:T(8,128)(2,1)}, bf16[1024,512]{0,1:T(8,128)(2,1)}) async-done(((bf16[1024,512]{0,1:T(8,128)(2,1)}, bf16[1024,512]{0,1:T(8,128)(2,1)}), (bf16[1024,512]{0,1:T(8,128)(2,1)}, bf16[1024,512]{0,1:T(8,128)(2,1)})) %all-reduce.4.cloned.1.call-update) | async-done | bytes 2097168 | tf_op jit(solution)/shard_map/psum | solution.py:14
  276.4 1.4 constant_dynamic-update-slice_fusion.1
  278.0 1.4 bitcast_dynamic-update-slice_fusion.7
  279.4 1.4 bitcast_dynamic-update-slice_fusion.6
  280.8 1.4 bitcast_dynamic-update-slice_fusion.5
  282.1 1.4 bitcast_dynamic-update-slice_fusion.4
  283.5 1.4 bitcast_dynamic-update-slice_fusion.3
  284.9 1.4 bitcast_dynamic-update-slice_fusion.2
  286.3 1.4 bitcast_dynamic-update-slice_fusion.1
  287.7 6.2 %copy-done.2 = f32[8,1024,512]{2,1,0:T(8,128)} copy-done((f32[8,1024,512]{2,1,0:T(8,128)}, f32[8,1024,512]{2,1,0:T(8,128)S(1)}, u32[]{:S(2)}) %copy-start.2) | copy-done | bytes 16777240
  293.8 2.7 bitcast_dynamic-update-slice_fusion
  (15 shorter events, 2.1 us)
Async XLA Ops:
  6.5 168.8 %all-gather.3.cloned.1.call-start = ((), (), s32[]{:S(2)}) async-start(), calls=%async_computation | async-start | bytes 10485760 | tf_op jit(solution)/shard_map/all_gather | solution.py:43
  84.9 191.4 %all-reduce.4.cloned.1.call-start = ((), (), s32[]{:S(2)}) async-start(), calls=%async_computation.1 | async-start | bytes 4194304 | tf_op jit(solution)/shard_map/psum | solution.py:14
  212.6 1.1 copy-start.1
  276.4 1.5 copy-start
  287.7 6.2 %copy-start.2 = (f32[8,1024,512]{2,1,0:T(8,128)}, f32[8,1024,512]{2,1,0:T(8,128)S(1)}, u32[]{:S(2)}) copy-start(f32[8,1024,512]{2,1,0:T(8,128)S(1)} %bitcast_dynamic-update-slice_fusion.1) | copy-start | bytes 50331652
Sparse Core Ops, SparseCore 0:
  85.1 90.1 all-gather.2
  213.8 62.5 all-reduce.3
